TPU v7x, 32 devices: a whole 2x2x4 slice. The times are simulated.
32 devices in a mesh: dp: 4 (over z), fsdp: 8 (over y, x, core).
Axes of the slice: x: 2, y: 2, z: 4, core: 2. Of those that a mesh axis runs over, the one named last changes fastest.
Arguments:
- frames: bfloat16 [256, 256, 512], P(('dp', 'fsdp')), may hold values from -6 to 6
- group: int32 [256], P(('dp', 'fsdp')), may hold values from 0 to 1
- lengths: int32 [256], P(('dp', 'fsdp')), may hold values from 128 to 256, as said below
- conv_weight: bfloat16 [2, 7, 512], P(None, None, ('dp', 'fsdp')), may hold values from -2 to 2
- conv_bias: bfloat16 [2, 512], P(None, ('dp', 'fsdp')), may hold values from -3 to 3
- ada_scale: bfloat16 [2, 2, 512], P(None, None, ('dp', 'fsdp')), may hold values from 0.5 to 1.5
- ada_shift: bfloat16 [2, 2, 512], P(None, None, ('dp', 'fsdp')), may hold values from -3 to 3
- up_weight: bfloat16 [2, 512, 1536], P(None, ('dp', 'fsdp')), may hold values from -0.25 to 0.25
- up_bias: bfloat16 [2, 1536], P(None, ('dp', 'fsdp')), may hold values from -3 to 3
- down_weight: bfloat16 [2, 1536, 512], P(None, ('dp', 'fsdp')), may hold values from -0.15625 to 0.15625
- down_bias: bfloat16 [2, 512], P(None, ('dp', 'fsdp')), may hold values from -3 to 3
- layer_scale: bfloat16 [2, 512], P(None, ('dp', 'fsdp')), may hold values from 0.5 to 1.5
- out_grad: bfloat16 [256, 256, 512], P(('dp', 'fsdp')), may hold values from -6 to 6
Outputs:
- output: bfloat16 [256, 256, 512], P(('dp', 'fsdp'))
- input_grad: float32 [256, 256, 512], P(('dp', 'fsdp'))
- conv_weight_grad: float32 [2, 7, 512], P(None, None, ('dp', 'fsdp'))
- conv_bias_grad: float32 [2, 512], P(None, ('dp', 'fsdp'))
- ada_scale_grad: float32 [2, 2, 512], P(None, None, ('dp', 'fsdp'))
- ada_shift_grad: float32 [2, 2, 512], P(None, None, ('dp', 'fsdp'))
- up_weight_grad: float32 [2, 512, 1536], P(None, ('dp', 'fsdp'))
- up_bias_grad: float32 [2, 1536], P(None, ('dp', 'fsdp'))
- down_weight_grad: float32 [2, 1536, 512], P(None, ('dp', 'fsdp'))
- down_bias_grad: float32 [2, 512], P(None, ('dp', 'fsdp'))
- layer_scale_grad: float32 [2, 512], P(None, ('dp', 'fsdp'))
Inputs may be any that keep to these rules, and one draw needn't show every extreme that they name: `lengths`: A clip of group 0 has at most 256 valid frames, one of group 1 at most 236; clip 0 has 256 and clip 1 has 236.
All inputs are finite; a program needn't handle non-finite values.
Results may differ from a plain program's by a relative error of at most 0.0066.
Values may be sent and summed in bfloat16 or wider, within the bound.
A program may use at most 192 MiB of HBM per device.

v0:
```python
from functools import partial
import jax
import jax.numpy as jnp
from jax import lax
from jax.sharding import PartitionSpec as P

EPSILON = 1e-06


def forward_block(fetched, stream, valid_rows, select):
    kernel_taps = fetched[0].astype(jnp.float32)
    conv_shift = fetched[1].astype(jnp.float32)
    scale_table = fetched[2].astype(jnp.float32)
    shift_table = fetched[3].astype(jnp.float32)
    up_matrix = fetched[4]
    up_offset = fetched[5].astype(jnp.float32)
    down_matrix = fetched[6]
    down_offset = fetched[7].astype(jnp.float32)
    layer_gain = fetched[8].astype(jnp.float32)
    clip_count, frame_count, model_width = stream.shape
    half_kernel = kernel_taps.shape[0] // 2
    masked = stream * valid_rows
    padded = jnp.pad(masked, ((0, 0), (half_kernel, half_kernel), (0, 0)))
    mixed = conv_shift
    for offset in range(kernel_taps.shape[0]):
        mixed = mixed + kernel_taps[offset] * padded[:, offset : offset + frame_count, :]
    center = mixed - jnp.mean(mixed, axis=-1, keepdims=True)
    spread = jnp.mean(center * center, axis=-1, keepdims=True)
    inv_std = lax.rsqrt(spread + EPSILON)
    normed = center * inv_std
    gain_rows = jnp.einsum("cg,gd->cd", select, scale_table, precision=lax.Precision.HIGHEST)
    shift_rows = jnp.einsum("cg,gd->cd", select, shift_table, precision=lax.Precision.HIGHEST)
    shaped = normed * gain_rows[:, None, :] + shift_rows[:, None, :]
    shaped_low = shaped.astype(jnp.bfloat16).reshape(clip_count * frame_count, model_width)
    before = jnp.dot(shaped_low, up_matrix, preferred_element_type=jnp.float32) + up_offset
    activated_low = jax.nn.gelu(before, approximate=False).astype(jnp.bfloat16)
    branch = jnp.dot(activated_low, down_matrix, preferred_element_type=jnp.float32) + down_offset
    branch = branch.reshape(clip_count, frame_count, model_width)
    output = stream + valid_rows * layer_gain * branch
    return (output, (padded, normed, inv_std, gain_rows, shaped_low, before, activated_low, branch))


def backward_block(fetched, saved_state, grad_stream, valid_rows, select):
    kernel_taps = fetched[0].astype(jnp.float32)
    up_matrix = fetched[4]
    down_matrix = fetched[6]
    layer_gain = fetched[8].astype(jnp.float32)
    padded, normed, inv_std, gain_rows, shaped_low, before, activated_low, branch = saved_state
    clip_count, frame_count, model_width = grad_stream.shape
    kernel_len = kernel_taps.shape[0]
    half_kernel = kernel_len // 2
    gain_term = jnp.sum(valid_rows * branch * grad_stream, axis=(0, 1))
    grad_branch = (valid_rows * layer_gain * grad_stream).astype(jnp.bfloat16)
    down_offset_term = jnp.sum(grad_branch.astype(jnp.float32), axis=(0, 1))
    branch_rows = grad_branch.reshape(clip_count * frame_count, model_width)
    down_term = jnp.einsum(
        "rh,rd->hd", activated_low, branch_rows, preferred_element_type=jnp.float32
    )
    grad_activated = jnp.einsum(
        "rd,hd->rh", branch_rows, down_matrix, preferred_element_type=jnp.float32
    )
    unused_value, gelu_pull = jax.vjp(partial(jax.nn.gelu, approximate=False), before)
    grad_before = gelu_pull(grad_activated)[0].astype(jnp.bfloat16)
    up_offset_term = jnp.sum(grad_before.astype(jnp.float32), axis=0)
    up_term = jnp.einsum("rd,rh->dh", shaped_low, grad_before, preferred_element_type=jnp.float32)
    grad_shaped = jnp.einsum(
        "rh,dh->rd", grad_before, up_matrix, preferred_element_type=jnp.float32
    )
    grad_shaped = grad_shaped.reshape(clip_count, frame_count, model_width)
    clip_scale = jnp.sum(grad_shaped * normed, axis=1)
    clip_shift = jnp.sum(grad_shaped, axis=1)
    scale_term = jnp.einsum("cg,cd->gd", select, clip_scale, precision=lax.Precision.HIGHEST)
    shift_term = jnp.einsum("cg,cd->gd", select, clip_shift, precision=lax.Precision.HIGHEST)
    grad_normed = grad_shaped * gain_rows[:, None, :]
    grad_mixed = inv_std * (
        grad_normed
        - jnp.mean(grad_normed, axis=-1, keepdims=True)
        - normed * jnp.mean(grad_normed * normed, axis=-1, keepdims=True)
    )
    conv_shift_term = jnp.sum(grad_mixed, axis=(0, 1))
    kernel_term = jnp.stack(
        [
            jnp.sum(grad_mixed * padded[:, offset : offset + frame_count, :], axis=(0, 1))
            for offset in range(kernel_len)
        ]
    )
    grad_padded = jnp.pad(grad_mixed, ((0, 0), (half_kernel, half_kernel), (0, 0)))
    grad_masked = jnp.zeros_like(grad_mixed)
    for offset in range(kernel_len):
        start_row = 2 * half_kernel - offset
        grad_masked = (
            grad_masked
            + kernel_taps[offset] * grad_padded[:, start_row : start_row + frame_count, :]
        )
    grad_input = grad_stream + valid_rows * grad_masked
    terms = (
        kernel_term,
        conv_shift_term,
        scale_term,
        shift_term,
        up_term,
        up_offset_term,
        down_term,
        down_offset_term,
        gain_term,
    )
    return (grad_input, terms)


def body(
    frames,
    group,
    lengths,
    conv_weight,
    conv_bias,
    ada_scale,
    ada_shift,
    up_weight,
    up_bias,
    down_weight,
    down_bias,
    layer_scale,
    out_grad,
):
    stream = frames.astype(jnp.float32)
    frame_count = stream.shape[1]
    block_count = conv_weight.shape[0]
    valid_rows = (jnp.arange(frame_count, dtype=jnp.int32)[None, :] < lengths[:, None]).astype(
        jnp.float32
    )[:, :, None]
    select = (group[:, None] == jnp.arange(ada_scale.shape[1], dtype=jnp.int32)[None, :]).astype(
        jnp.float32
    )
    saved_states = []
    for block_index in range(block_count):
        fetched = (
            lax.all_gather(conv_weight[block_index], ("dp", "fsdp"), axis=1, tiled=True),
            lax.all_gather(conv_bias[block_index], ("dp", "fsdp"), axis=0, tiled=True),
            lax.all_gather(ada_scale[block_index], ("dp", "fsdp"), axis=1, tiled=True),
            lax.all_gather(ada_shift[block_index], ("dp", "fsdp"), axis=1, tiled=True),
            lax.all_gather(up_weight[block_index], ("dp", "fsdp"), axis=0, tiled=True),
            lax.all_gather(up_bias[block_index], ("dp", "fsdp"), axis=0, tiled=True),
            lax.all_gather(down_weight[block_index], ("dp", "fsdp"), axis=0, tiled=True),
            lax.all_gather(down_bias[block_index], ("dp", "fsdp"), axis=0, tiled=True),
            lax.all_gather(layer_scale[block_index], ("dp", "fsdp"), axis=0, tiled=True),
        )
        stream, block_state = forward_block(fetched, stream, valid_rows, select)
        saved_states.append(block_state)
    output = stream.astype(jnp.bfloat16)
    grad_stream = out_grad.astype(jnp.float32)
    shard_lists = [None] * block_count
    for block_index in reversed(range(block_count)):
        fetched = (
            lax.all_gather(conv_weight[block_index], ("dp", "fsdp"), axis=1, tiled=True),
            lax.all_gather(conv_bias[block_index], ("dp", "fsdp"), axis=0, tiled=True),
            lax.all_gather(ada_scale[block_index], ("dp", "fsdp"), axis=1, tiled=True),
            lax.all_gather(ada_shift[block_index], ("dp", "fsdp"), axis=1, tiled=True),
            lax.all_gather(up_weight[block_index], ("dp", "fsdp"), axis=0, tiled=True),
            lax.all_gather(up_bias[block_index], ("dp", "fsdp"), axis=0, tiled=True),
            lax.all_gather(down_weight[block_index], ("dp", "fsdp"), axis=0, tiled=True),
            lax.all_gather(down_bias[block_index], ("dp", "fsdp"), axis=0, tiled=True),
            lax.all_gather(layer_scale[block_index], ("dp", "fsdp"), axis=0, tiled=True),
        )
        grad_stream, terms = backward_block(
            fetched, saved_states[block_index], grad_stream, valid_rows, select
        )
        shards = (
            lax.psum_scatter(terms[0], ("dp", "fsdp"), scatter_dimension=1, tiled=True),
            lax.psum_scatter(terms[1], ("dp", "fsdp"), scatter_dimension=0, tiled=True),
            lax.psum_scatter(terms[2], ("dp", "fsdp"), scatter_dimension=1, tiled=True),
            lax.psum_scatter(terms[3], ("dp", "fsdp"), scatter_dimension=1, tiled=True),
            lax.psum_scatter(terms[4], ("dp", "fsdp"), scatter_dimension=0, tiled=True),
            lax.psum_scatter(terms[5], ("dp", "fsdp"), scatter_dimension=0, tiled=True),
            lax.psum_scatter(terms[6], ("dp", "fsdp"), scatter_dimension=0, tiled=True),
            lax.psum_scatter(terms[7], ("dp", "fsdp"), scatter_dimension=0, tiled=True),
            lax.psum_scatter(terms[8], ("dp", "fsdp"), scatter_dimension=0, tiled=True),
        )
        shard_lists[block_index] = shards
    stacked = tuple(
        (
            jnp.stack([shard_lists[block_index][entry] for block_index in range(block_count)])
            for entry in range(9)
        )
    )
    return (
        output,
        grad_stream,
        stacked[0],
        stacked[1],
        stacked[2],
        stacked[3],
        stacked[4],
        stacked[5],
        stacked[6],
        stacked[7],
        stacked[8],
    )


def solution(mesh):
    in_specs = (
        P(("dp", "fsdp"), None, None),
        P(("dp", "fsdp")),
        P(("dp", "fsdp")),
        P(None, None, ("dp", "fsdp")),
        P(None, ("dp", "fsdp")),
        P(None, None, ("dp", "fsdp")),
        P(None, None, ("dp", "fsdp")),
        P(None, ("dp", "fsdp"), None),
        P(None, ("dp", "fsdp")),
        P(None, ("dp", "fsdp"), None),
        P(None, ("dp", "fsdp")),
        P(None, ("dp", "fsdp")),
        P(("dp", "fsdp"), None, None),
    )
    out_specs = (
        P(("dp", "fsdp"), None, None),
        P(("dp", "fsdp"), None, None),
        P(None, None, ("dp", "fsdp")),
        P(None, ("dp", "fsdp")),
        P(None, None, ("dp", "fsdp")),
        P(None, None, ("dp", "fsdp")),
        P(None, ("dp", "fsdp"), None),
        P(None, ("dp", "fsdp")),
        P(None, ("dp", "fsdp"), None),
        P(None, ("dp", "fsdp")),
        P(None, ("dp", "fsdp")),
    )
    return jax.shard_map(body, mesh=mesh, in_specs=in_specs, out_specs=out_specs, check_vma=False)
```

profile of v0, /device:TPU:0, one launch (start us, length us, event | category | flops | bytes accessed | tf_op | source)
XLA Modules:
  0.0 1740.9 jit_solution(17593879401863547179)
XLA Ops:
  16.5 42.2 %all-reduce.21 = (bf16[512]{0:T(512)(128)(2,1)S(1)}, bf16[1536]{0:T(1024)(128)(2,1)S(1)}, bf16[512]{0:T(512)(128)(2,1)S(1)}, bf16[512]{0:T(512)(128)(2,1)S(1)}, ...) all-reduce(bf16[512]{0:T(512)(128)(2,1)S(1)} %dynamic-update-slice., ...), channel_id=3, replica_groups=mesh['dp'=4,'fsdp'=8] {'dp','fsdp'}, use_global_device_ids=true, to_apply=%add.5 | all-reduce | flops 6144 | bytes 24576
  59.6 41.4 %all-gather.2 = bf16[1,7,512]{1,0,2:T(2,128)(2,1)S(1)} all-gather(bf16[1,7,16]{1,0,2:T(2,128)(2,1)S(1)} %copy.55), channel_id=4, replica_groups=mesh['dp'=4,'fsdp'=8] {'dp','fsdp'}, dimensions={2}, use_global_device_ids=true | all-gather | bytes 7392 | tf_op jit(solution)/shard_map/all_gather | solution.py:137
  123.8 37.3 %all-gather.3 = bf16[1,2,512]{1,0,2:T(2,128)(2,1)S(1)} all-gather(bf16[1,2,16]{1,0,2:T(2,128)(2,1)S(1)} %copy.56), channel_id=5, replica_groups=mesh['dp'=4,'fsdp'=8] {'dp','fsdp'}, dimensions={2}, use_global_device_ids=true | all-gather | bytes 2112 | tf_op jit(solution)/shard_map/all_gather | solution.py:139
  161.4 38.8 %all-gather.4 = bf16[1,2,512]{1,0,2:T(2,128)(2,1)S(1)} all-gather(bf16[1,2,16]{1,0,2:T(2,128)(2,1)S(1)} %copy.57), channel_id=6, replica_groups=mesh['dp'=4,'fsdp'=8] {'dp','fsdp'}, dimensions={2}, use_global_device_ids=true | all-gather | bytes 2112 | tf_op jit(solution)/shard_map/all_gather | solution.py:140
  200.9 37.7 %all-gather.11 = bf16[1,7,512]{1,0,2:T(2,128)(2,1)S(1)} all-gather(bf16[1,7,16]{1,0,2:T(2,128)(2,1)S(1)} %copy.58), channel_id=13, replica_groups=mesh['dp'=4,'fsdp'=8] {'dp','fsdp'}, dimensions={2}, use_global_device_ids=true | all-gather | bytes 7392 | tf_op jit(solution)/shard_map/all_gather | solution.py:137
  253.0 38.5 %all-gather.12 = bf16[1,2,512]{1,0,2:T(2,128)(2,1)S(1)} all-gather(bf16[1,2,16]{1,0,2:T(2,128)(2,1)S(1)} %copy.59), channel_id=14, replica_groups=mesh['dp'=4,'fsdp'=8] {'dp','fsdp'}, dimensions={2}, use_global_device_ids=true | all-gather | bytes 2112 | tf_op jit(solution)/shard_map/all_gather | solution.py:139
  292.0 37.6 %all-gather.13 = bf16[1,2,512]{1,0,2:T(2,128)(2,1)S(1)} all-gather(bf16[1,2,16]{1,0,2:T(2,128)(2,1)S(1)} %copy.60), channel_id=15, replica_groups=mesh['dp'=4,'fsdp'=8] {'dp','fsdp'}, dimensions={2}, use_global_device_ids=true | all-gather | bytes 2112 | tf_op jit(solution)/shard_map/all_gather | solution.py:140
  334.2 33.1 %multiply_convert_fusion.1 = (bf16[2048,1536]{1,0:T(8,128)(2,1)}, f32[2048,1536]{1,0:T(8,128)}, f32[2048,1536]{1,0:T(8,128)}) fusion(f32[1536]{0:T(1024)S(1)} %convert_element_type.134, bf16[2048,512]{1,0:T(8,128)(2,1)} %bitcast.165, bf16[1,512,1536]{2,1,0:T(8,128)(2,1)} %all-gather.23.cloned.1.call-done), kind=kOutput, calls=%fused_computation.21 | convolution fusion | flops 3428843520 | bytes 35133440 | tf_op jit(solution)/shard_map/dot_general | solution.py:35
  383.3 34.2 %multiply_convert_fusion = (bf16[2048,1536]{1,0:T(8,128)(2,1)}, f32[2048,1536]{1,0:T(8,128)}, f32[2048,1536]{1,0:T(8,128)}) fusion(f32[1536]{0:T(1024)S(1)} %convert_element_type.138, bf16[2048,512]{1,0:T(8,128)(2,1)S(1)} %bitcast.167, bf16[1,512,1536]{2,1,0:T(8,128)(2,1)} %all-gather.27.cloned.1.call-done), kind=kOutput, calls=%fused_computation.8 | convolution fusion | flops 3428843520 | bytes 35133440 | tf_op jit(solution)/shard_map/dot_general | solution.py:35
  438.3 20.4 %multiply_reduce_fusion.3 = (f32[512]{0:T(512)S(1)}, f32[512]{0:T(512)S(1)}, f32[512]{0:T(512)S(1)}, f32[512]{0:T(512)S(1)}, f32[512]{0:T(512)S(1)}, /*index=5*/...) fusion(f32[8,256,512]{2,1,0:T(8,128)} %copy-done.9, ...), kind=kLoop, calls=%fused_computation.60 | loop fusion | flops 23064576 | bytes 16842752 | tf_op jit(solution)/shard_map/reduce_sum | solution.py:83
  466.8 20.3 %convert_reduce_fusion.3 = (f32[512]{0:T(512)S(1)}, bf16[8,256,512]{2,1,0:T(8,128)(2,1)}, f32[8,256,512]{2,1,0:T(8,128)}, bf16[8,256,512]{2,1,0:T(8,128)(2,1)}) fusion(f32[512]{0:T(512)S(1)} %convert_element_type.132, f32[8,256]{1,0:T(8,128)S(1)} %fusion.38, f32[512]{0:T(512)S(1)} %get-tuple-element.72, f32[512]{0:T(512)S(1)} %get-tuple-element.67, ...), kind=kLoop, calls=%fused_computation.57 | loop fusion | flops 29359616 | bytes 25194496 | tf_op jit(solution)/shard_map/reduce_sum | solution.py:54
  487.1 14.9 convert_reduce_fusion.1
  514.3 23.7 %multiply_reduce_fusion.10 = (f32[512]{0:T(512)S(1)}, f32[512]{0:T(512)S(1)}, f32[512]{0:T(512)S(1)}, f32[512]{0:T(512)S(1)}, f32[512]{0:T(512)S(1)}, /*index=5*...) fusion(f32[8,256,512]{2,1,0:T(8,128)} %copy-done.6, ...), kind=kLoop, calls=%fused_computation.67 | loop fusion | flops 32500736 | bytes 33632256 | tf_op jit(solution)/shard_map/reduce_sum | solution.py:83
  573.7 37.3 %all-reduce.20 = (f32[512]{0:T(512)S(1)}, f32[512]{0:T(512)S(1)}, f32[1536]{0:T(1024)S(1)}, f32[1536]{0:T(1024)S(1)}, f32[512]{0:T(512)S(1)}, /*index=5*/f32[512]{0:T(512)S(1)}, f32[512]{0:T(512)S(1)}, f32[512]{0:T(512)S(1)}) all-reduce(f32[512]{0:T(512)S(1)} %get-tuple-element.64, ...), channel_id=23, replica_groups=mesh['dp'=4,'fsdp'=8] {'dp','fsdp'}, use_global_device_ids=true, to_apply=%region_27.28.clone | all-reduce | flops 6144 | bytes 49152
  613.7 18.2 %multiply_add_fusion = f32[8,256,512]{2,1,0:T(8,128)} fusion(f32[8,256,512]{2,1,0:T(8,128)} %get-tuple-element.100, f32[8,256,512]{2,1,0:T(8,128)} %get-tuple-element.103, f32[512]{0:T(512)S(1)} %copy-done.39, f32[512]{0:T(512)S(1)} %copy-done.29, f32[512]{0:T(512)S(1)} %copy-done.31, f32[512]{0:T(512)S(1)} %copy-done.33, f32[512]{0:T(512)S(1)} %copy-done.35, ...), kind=kLoop, calls=%fused_computation.74 | loop fusion | flops 15728640 | bytes 12605440 | tf_op jit(solution)/shard_map/add | solution.py:95
  643.1 132.8 %reduce-scatter.39.cloned.1.call-done = f32[16,2]{1,0:T(8,128)} async-done(((f32[512,2]{1,0:T(8,128)}), f32[16,2]{1,0:T(8,128)}) %reduce-scatter.39.cloned.1.call-update) | async-done | bytes 144
  776.7 133.0 %reduce-scatter.37.cloned.1.call-done = f32[16,2]{1,0:T(8,128)} async-done(((f32[512,2]{1,0:T(8,128)}), f32[16,2]{1,0:T(8,128)}) %reduce-scatter.37.cloned.1.call-update) | async-done | bytes 144
  910.4 132.6 %reduce-scatter.41.cloned.1.call-done = f32[16,2]{1,0:T(8,128)} async-done(((f32[512,2]{1,0:T(8,128)}), f32[16,2]{1,0:T(8,128)}) %reduce-scatter.41.cloned.1.call-update) | async-done | bytes 144
  1044.4 132.0 %reduce-scatter.31.cloned.1.call-done = f32[16,7]{1,0:T(8,128)} async-done(((f32[512,7]{1,0:T(8,128)}), f32[16,7]{1,0:T(8,128)}) %reduce-scatter.31.cloned.1.call-update) | async-done | bytes 464
  1177.1 132.4 %reduce-scatter.33.cloned.1.call-done = f32[16,7]{1,0:T(8,128)} async-done(((f32[512,7]{1,0:T(8,128)}), f32[16,7]{1,0:T(8,128)}) %reduce-scatter.33.cloned.1.call-update) | async-done | bytes 464
  1310.9 102.1 %reduce-scatter.27.cloned.1.call-done = f32[48,512]{1,0:T(8,128)} async-done(((f32[1536,512]{1,0:T(8,128)}), f32[48,512]{1,0:T(8,128)}) %reduce-scatter.27.cloned.1.call-update) | async-done | bytes 98320 | tf_op jit(solution)/shard_map/reduce_scatter | solution.py:174
  1413.0 106.4 %reduce-scatter.29.cloned.1.call-done = f32[48,512]{1,0:T(8,128)} async-done(((f32[1536,512]{1,0:T(8,128)}), f32[48,512]{1,0:T(8,128)}) %reduce-scatter.29.cloned.1.call-update) | async-done | bytes 98320 | tf_op jit(solution)/shard_map/reduce_scatter | solution.py:174
  1521.0 105.0 %reduce-scatter.25.cloned.1.call-done = f32[16,1536]{1,0:T(8,128)} async-done(((f32[512,1536]{1,0:T(8,128)}), f32[16,1536]{1,0:T(8,128)}) %reduce-scatter.25.cloned.1.call-update) | async-done | bytes 98320 | tf_op jit(solution)/shard_map/reduce_scatter | solution.py:172
  1626.0 106.5 %reduce-scatter.23.cloned.1.call-done = f32[16,1536]{1,0:T(8,128)} async-done(((f32[512,1536]{1,0:T(8,128)}), f32[16,1536]{1,0:T(8,128)}) %reduce-scatter.23.cloned.1.call-update) | async-done | bytes 98320 | tf_op jit(solution)/shard_map/reduce_scatter | solution.py:172
  (235 shorter events, 167.5 us)
Async XLA Ops:
  7.2 109.0 %copy-start.10 = (bf16[8,256,512]{2,1,0:T(8,128)(2,1)S(1)}, bf16[8,256,512]{2,1,0:T(8,128)(2,1)}, u32[]{:S(2)}) copy-start(bf16[8,256,512]{2,1,0:T(8,128)(2,1)} %param.13) | copy-start | bytes 6291460
  7.2 327.0 %all-gather.23.cloned.1.call-start = ((), (), s32[]{:S(2)}) async-start(), calls=%async_computation.14 | async-start | bytes 1622016 | tf_op jit(solution)/shard_map/all_gather | solution.py:141
  8.9 358.5 %all-gather.25.cloned.1.call-start = ((), (), s32[]{:S(2)}) async-start(), calls=%async_computation.15 | async-start | bytes 1622016 | tf_op jit(solution)/shard_map/all_gather | solution.py:143
  10.4 372.9 %all-gather.27.cloned.1.call-start = ((), (), s32[]{:S(2)}) async-start(), calls=%async_computation.16 | async-start | bytes 1622016 | tf_op jit(solution)/shard_map/all_gather | solution.py:141
  11.1 406.4 %all-gather.29.cloned.1.call-start = ((), (), s32[]{:S(2)}) async-start(), calls=%async_computation.17 | async-start | bytes 1622016 | tf_op jit(solution)/shard_map/all_gather | solution.py:143
  11.7 630.6 %reduce-scatter.35.cloned.1.call-start = ((), (), s32[]{:S(2)}) async-start(), calls=%async_computation.20 | async-start | bytes 270336
  120.9 79.4 %copy-start.40 = (s32[8]{0:T(128)S(1)}, s32[8]{0:T(128)}, u32[]{:S(2)}) copy-start(s32[8]{0:T(128)} %param.14) | copy-start | bytes 100
  120.9 209.6 %copy-start.22 = (f32[8,256]{1,0:T(8,128)}, f32[8,256]{1,0:T(8,128)S(1)}, u32[]{:S(2)}) copy-start(f32[8,256]{1,0:T(8,128)S(1)} %broadcast_multiply_fusion.5) | copy-start | bytes 24580
  123.7 210.4 %copy-start.24 = (f32[8,256]{1,0:T(8,128)}, f32[8,256]{1,0:T(8,128)S(1)}, u32[]{:S(2)}) copy-start(f32[8,256]{1,0:T(8,128)S(1)} %add_rsqrt_fusion.1) | copy-start | bytes 24580
  200.5 133.6 %copy-start.20 = (f32[8,512]{1,0:T(8,128)}, f32[8,512]{1,0:T(8,128)S(1)}, u32[]{:S(2)}) copy-start(f32[8,512]{1,0:T(8,128)S(1)} %fusion.42) | copy-start | bytes 49156
  509.2 266.7 %reduce-scatter.39.cloned.1.call-start = ((), (), s32[]{:S(2)}) async-start(), calls=%async_computation.22 | async-start | bytes 270336
  512.7 397.0 %reduce-scatter.37.cloned.1.call-start = ((), (), s32[]{:S(2)}) async-start(), calls=%async_computation.21 | async-start | bytes 270336
  513.5 529.6 %reduce-scatter.41.cloned.1.call-start = ((), (), s32[]{:S(2)}) async-start(), calls=%async_computation.23 | async-start | bytes 270336
  514.2 662.1 %reduce-scatter.31.cloned.1.call-start = ((), (), s32[]{:S(2)}) async-start(), calls=%async_computation.18 | async-start | bytes 270336
  538.9 770.6 %reduce-scatter.33.cloned.1.call-start = ((), (), s32[]{:S(2)}) async-start(), calls=%async_computation.19 | async-start | bytes 270336
  539.9 873.1 %reduce-scatter.27.cloned.1.call-start = ((), (), s32[]{:S(2)}) async-start(), calls=%async_computation.12 | async-start | bytes 3244032 | tf_op jit(solution)/shard_map/reduce_scatter | solution.py:174
  548.7 970.7 %reduce-scatter.29.cloned.1.call-start = ((), (), s32[]{:S(2)}) async-start(), calls=%async_computation.13 | async-start | bytes 3244032 | tf_op jit(solution)/shard_map/reduce_scatter | solution.py:174
  556.8 1069.2 %reduce-scatter.25.cloned.1.call-start = ((), (), s32[]{:S(2)}) async-start(), calls=%async_computation.11 | async-start | bytes 3244032 | tf_op jit(solution)/shard_map/reduce_scatter | solution.py:172
  565.6 48.0 %copy-start.27 = (f32[512]{0:T(512)S(1)}, f32[512]{0:T(512)}, u32[]{:S(2)}) copy-start(f32[512]{0:T(512)} %copy-done.26) | copy-start | bytes 6148
  565.6 48.0 %copy-start.29 = (f32[512]{0:T(512)S(1)}, f32[512]{0:T(512)}, u32[]{:S(2)}) copy-start(f32[512]{0:T(512)} %copy-done.28) | copy-start | bytes 6148
  565.6 48.0 %copy-start.31 = (f32[512]{0:T(512)S(1)}, f32[512]{0:T(512)}, u32[]{:S(2)}) copy-start(f32[512]{0:T(512)} %copy-done.30) | copy-start | bytes 6148
  565.6 48.0 %copy-start.33 = (f32[512]{0:T(512)S(1)}, f32[512]{0:T(512)}, u32[]{:S(2)}) copy-start(f32[512]{0:T(512)} %copy-done.32) | copy-start | bytes 6148
  565.7 48.0 %copy-start.35 = (f32[512]{0:T(512)S(1)}, f32[512]{0:T(512)}, u32[]{:S(2)}) copy-start(f32[512]{0:T(512)} %copy-done.34) | copy-start | bytes 6148
  565.7 1166.8 %reduce-scatter.23.cloned.1.call-start = ((), (), s32[]{:S(2)}) async-start(), calls=%async_computation.10 | async-start | bytes 3244032 | tf_op jit(solution)/shard_map/reduce_scatter | solution.py:172
  (37 other events, 391.8 us)
Sparse Core Ops, SparseCore 0:
  11.4 57.6 all-gather.22
  72.0 54.0 all-gather.24
  129.5 54.0 all-gather.26
  186.9 54.2 all-gather.28
  509.3 132.9 reduce-scatter.34
  644.4 131.4 reduce-scatter.38
  778.1 131.4 reduce-scatter.36
  911.9 131.0 reduce-scatter.40
  1045.3 131.0 reduce-scatter.30
  1178.4 131.0 reduce-scatter.32
  1315.0 98.0 reduce-scatter.26
  1418.3 101.0 reduce-scatter.28
  1524.8 101.1 reduce-scatter.24
  1631.3 101.1 reduce-scatter.22
where the time goes:
time: 1740 us
  waiting for transfers between devices  1100 us (63%)
  blocking collectives  311 us (18%)
  matrix products  157 us (9%)
  other arithmetic  111 us (6%)
  local copies, waits for them, and re-layouts  50.3 us (3%)
    unnamed x20, waiting for transfers between devices  676 us
    reduce_scatter x2, waiting for transfers between devices, body(): lax.psum_scatter(terms[4], ('dp', 'fsdp'), scatter_dimension=0, tiled=True)  211 us
    reduce_scatter x2, waiting for transfers between devices, body(): lax.psum_scatter(terms[6], ('dp', 'fsdp'), scatter_dimension=0, tiled=True)  208 us
    unnamed x2, blocking collectives  79.5 us
    all_gather x2, blocking collectives, body(): lax.all_gather(conv_weight[block_index], ('dp', 'fsdp'), axis=1, tiled=True)  79 us
    all_gather x2, blocking collectives, body(): lax.all_gather(ada_shift[block_index], ('dp', 'fsdp'), axis=1, tiled=True)  76.5 us
    all_gather x2, blocking collectives, body(): lax.all_gather(ada_scale[block_index], ('dp', 'fsdp'), axis=1, tiled=True)  75.8 us
    dot_general x2, matrix products, forward_block(): jnp.dot(shaped_low, up_matrix, preferred_element_type=jnp.float32)  67.3 us
  transfers between devices with their start and end apart: 14, of which 10 were waited for; matrix products, arithmetic and copies ran while one was open for 13% of the time, Pallas kernels for 0%

commit v1 on v0

--- a/solution.py
+++ b/solution.py
@@ -5,6 +5,26 @@
 from jax.sharding import PartitionSpec as P
 
 EPSILON = 1e-06
+
+
+def _produce_trees(x_local, along_dim):
+    main = list(x_local.shape[1:])
+    main[along_dim] *= x_local.shape[0]
+    return jnp.moveaxis(x_local, 0, along_dim).reshape(main)
+
+
+def group_edges_on_mesh(tile_in, named_axis):
+    size_here = lax.axis_size(named_axis)
+    then = tile_in[None]
+    for ii in range(size_here.bit_length() - 1):
+        response = 1 << ii
+        current_value = lax.ppermute(
+            then, axis_name=named_axis, perm=[(p, p ^ response) for p in range(size_here)]
+        )
+        z = jnp.stack([then, current_value], 0)
+        far_arr = lax.axis_index(named_axis) >> ii & 1
+        then = jnp.where(far_arr == 0, z, z[::-1]).reshape(-1, *tile_in.shape)
+    return then
 
 
 def forward_block(fetched, stream, valid_rows, select):
@@ -133,11 +153,15 @@
     )
     saved_states = []
     for block_index in range(block_count):
+
+        def _bring_scales(view, incoming_x, dim_k):
+            return _produce_trees(group_edges_on_mesh(view, incoming_x), dim_k)
+
         fetched = (
             lax.all_gather(conv_weight[block_index], ("dp", "fsdp"), axis=1, tiled=True),
             lax.all_gather(conv_bias[block_index], ("dp", "fsdp"), axis=0, tiled=True),
             lax.all_gather(ada_scale[block_index], ("dp", "fsdp"), axis=1, tiled=True),
-            lax.all_gather(ada_shift[block_index], ("dp", "fsdp"), axis=1, tiled=True),
+            _bring_scales(ada_shift[block_index], ("dp", "fsdp"), dim_k=1),
             lax.all_gather(up_weight[block_index], ("dp", "fsdp"), axis=0, tiled=True),
             lax.all_gather(up_bias[block_index], ("dp", "fsdp"), axis=0, tiled=True),
             lax.all_gather(down_weight[block_index], ("dp", "fsdp"), axis=0, tiled=True),

time: 1740 us -> 1690 us (0.971)
  blocking collectives: 311 us -> 237 us
    all_gather x2 -> x0, blocking collectives: 76.5 us -> none  [body(): lax.all_gather(ada_shift[block_index], ('dp', 'fsdp'), axis=1, tiled=True)]
  transfers between devices with their start and end apart: 14 -> 24, of which waited for: 10 -> 18; matrix products, arithmetic and copies ran while one was open for 13% -> 13% of each run, Pallas kernels for 0% -> 0%
where the time goes in v1:
time: 1690 us; the launch traced here: 1680 us
  waiting for transfers between devices  1110 us (66%)
  blocking collectives  237 us (14%)
  matrix products  157 us (9%)
  other arithmetic  112 us (7%)
  local copies, waits for them, and re-layouts  50.7 us (3%)
    unnamed x20, waiting for transfers between devices  676 us
    reduce_scatter x2, waiting for transfers between devices, body(): lax.psum_scatter(terms[4], ('dp', 'fsdp'), scatter_dimension=0, tiled=True)  211 us
    reduce_scatter x2, waiting for transfers between devices, body(): lax.psum_scatter(terms[6], ('dp', 'fsdp'), scatter_dimension=0, tiled=True)  208 us
    unnamed x2, blocking collectives  81.2 us
    all_gather x2, blocking collectives, body(): lax.all_gather(conv_weight[block_index], ('dp', 'fsdp'), axis=1, tiled=True)  79.9 us
    all_gather x2, blocking collectives, body(): lax.all_gather(ada_scale[block_index], ('dp', 'fsdp'), axis=1, tiled=True)  75.6 us
    dot_general x2, matrix products, forward_block(): jnp.dot(shaped_low, up_matrix, preferred_element_type=jnp.float32)  67.3 us
    reduce_sum x2, other arithmetic, backward_block(): jnp.sum(grad_mixed * padded[:, offset:offset + frame_count, :], axis=(0, 1))  44.2 us
  transfers between devices with their start and end apart: 24, of which 18 were waited for; matrix products, arithmetic and copies ran while one was open for 13% of the time, Pallas kernels for 0%

profile of v1, /device:TPU:0, one launch (start us, length us, event | category | flops | bytes accessed | tf_op | source)
XLA Modules:
  0.0 1684.4 jit_solution(16016116655598984602)
XLA Ops:
  17.2 42.3 %all-reduce.21 = (bf16[512]{0:T(512)(128)(2,1)S(1)}, bf16[1536]{0:T(1024)(128)(2,1)S(1)}, bf16[512]{0:T(512)(128)(2,1)S(1)}, bf16[512]{0:T(512)(128)(2,1)S(1)}, ...) all-reduce(bf16[512]{0:T(512)(128)(2,1)S(1)} %dynamic-update-slice., ...), channel_id=3, replica_groups=mesh['dp'=4,'fsdp'=8] {'dp','fsdp'}, use_global_device_ids=true, to_apply=%add.5 | all-reduce | flops 6144 | bytes 24576
  60.3 41.4 %all-gather.2 = bf16[1,7,512]{1,0,2:T(2,128)(2,1)S(1)} all-gather(bf16[1,7,16]{1,0,2:T(2,128)(2,1)S(1)} %copy.62), channel_id=4, replica_groups=mesh['dp'=4,'fsdp'=8] {'dp','fsdp'}, dimensions={2}, use_global_device_ids=true | all-gather | bytes 7392 | tf_op jit(solution)/shard_map/all_gather | solution.py:161
  102.0 14.1 slice_reduce_fusion.13
  124.6 37.6 %all-gather.3 = bf16[1,2,512]{1,0,2:T(2,128)(2,1)S(1)} all-gather(bf16[1,2,16]{1,0,2:T(2,128)(2,1)S(1)} %copy.63), channel_id=5, replica_groups=mesh['dp'=4,'fsdp'=8] {'dp','fsdp'}, dimensions={2}, use_global_device_ids=true | all-gather | bytes 2112 | tf_op jit(solution)/shard_map/all_gather | solution.py:163
  162.5 38.5 %all-gather.10 = bf16[1,7,512]{1,0,2:T(2,128)(2,1)S(1)} all-gather(bf16[1,7,16]{1,0,2:T(2,128)(2,1)S(1)} %copy.64), channel_id=12, replica_groups=mesh['dp'=4,'fsdp'=8] {'dp','fsdp'}, dimensions={2}, use_global_device_ids=true | all-gather | bytes 7392 | tf_op jit(solution)/shard_map/all_gather | solution.py:161
  215.5 38.0 %all-gather.11 = bf16[1,2,512]{1,0,2:T(2,128)(2,1)S(1)} all-gather(bf16[1,2,16]{1,0,2:T(2,128)(2,1)S(1)} %copy.65), channel_id=13, replica_groups=mesh['dp'=4,'fsdp'=8] {'dp','fsdp'}, dimensions={2}, use_global_device_ids=true | all-gather | bytes 2112 | tf_op jit(solution)/shard_map/all_gather | solution.py:163
  275.8 33.1 %multiply_convert_fusion.1 = (bf16[2048,1536]{1,0:T(8,128)(2,1)}, f32[2048,1536]{1,0:T(8,128)}, f32[2048,1536]{1,0:T(8,128)}) fusion(f32[1536]{0:T(1024)S(1)} %convert_element_type.134, bf16[2048,512]{1,0:T(8,128)(2,1)} %bitcast.201, bf16[1,512,1536]{2,1,0:T(8,128)(2,1)} %all-gather.21.cloned.1.call-done), kind=kOutput, calls=%fused_computation.21 | convolution fusion | flops 3428843520 | bytes 35133440 | tf_op jit(solution)/shard_map/dot_general | solution.py:55
  324.9 34.2 %multiply_convert_fusion = (bf16[2048,1536]{1,0:T(8,128)(2,1)}, f32[2048,1536]{1,0:T(8,128)}, f32[2048,1536]{1,0:T(8,128)}) fusion(f32[1536]{0:T(1024)S(1)} %convert_element_type.138, bf16[2048,512]{1,0:T(8,128)(2,1)S(1)} %bitcast.203, bf16[1,512,1536]{2,1,0:T(8,128)(2,1)} %all-gather.25.cloned.1.call-done), kind=kOutput, calls=%fused_computation.8 | convolution fusion | flops 3428843520 | bytes 35133440 | tf_op jit(solution)/shard_map/dot_general | solution.py:55
  359.1 14.7 convert_reduce_fusion
  379.9 20.4 %multiply_reduce_fusion.3 = (f32[512]{0:T(512)S(1)}, f32[512]{0:T(512)S(1)}, f32[512]{0:T(512)S(1)}, f32[512]{0:T(512)S(1)}, f32[512]{0:T(512)S(1)}, /*index=5*/...) fusion(f32[8,256,512]{2,1,0:T(8,128)} %copy-done.9, ...), kind=kLoop, calls=%fused_computation.60 | loop fusion | flops 23064576 | bytes 16842752 | tf_op jit(solution)/shard_map/reduce_sum | solution.py:103
  408.4 20.3 %convert_reduce_fusion.3 = (f32[512]{0:T(512)S(1)}, bf16[8,256,512]{2,1,0:T(8,128)(2,1)}, f32[8,256,512]{2,1,0:T(8,128)}, bf16[8,256,512]{2,1,0:T(8,128)(2,1)}) fusion(f32[512]{0:T(512)S(1)} %convert_element_type.132, f32[8,256]{1,0:T(8,128)S(1)} %fusion.38, f32[512]{0:T(512)S(1)} %get-tuple-element.83, f32[512]{0:T(512)S(1)} %get-tuple-element.78, ...), kind=kLoop, calls=%fused_computation.57 | loop fusion | flops 29359616 | bytes 25194496 | tf_op jit(solution)/shard_map/reduce_sum | solution.py:74
  428.7 14.9 convert_reduce_fusion.1
  455.9 23.7 %multiply_reduce_fusion.10 = (f32[512]{0:T(512)S(1)}, f32[512]{0:T(512)S(1)}, f32[512]{0:T(512)S(1)}, f32[512]{0:T(512)S(1)}, f32[512]{0:T(512)S(1)}, /*index=5*...) fusion(f32[8,256,512]{2,1,0:T(8,128)} %copy-done.6, ...), kind=kLoop, calls=%fused_computation.67 | loop fusion | flops 32500736 | bytes 33632256 | tf_op jit(solution)/shard_map/reduce_sum | solution.py:103
  515.3 38.9 %all-reduce.20 = (f32[512]{0:T(512)S(1)}, f32[512]{0:T(512)S(1)}, f32[1536]{0:T(1024)S(1)}, f32[1536]{0:T(1024)S(1)}, f32[512]{0:T(512)S(1)}, /*index=5*/f32[512]{0:T(512)S(1)}, f32[512]{0:T(512)S(1)}, f32[512]{0:T(512)S(1)}) all-reduce(f32[512]{0:T(512)S(1)} %get-tuple-element.75, ...), channel_id=21, replica_groups=mesh['dp'=4,'fsdp'=8] {'dp','fsdp'}, use_global_device_ids=true, to_apply=%region_27.28.clone | all-reduce | flops 6144 | bytes 49152
  556.9 18.2 %multiply_add_fusion = f32[8,256,512]{2,1,0:T(8,128)} fusion(f32[8,256,512]{2,1,0:T(8,128)} %get-tuple-element.111, f32[8,256,512]{2,1,0:T(8,128)} %get-tuple-element.114, f32[512]{0:T(512)S(1)} %copy-done.39, f32[512]{0:T(512)S(1)} %copy-done.29, f32[512]{0:T(512)S(1)} %copy-done.31, f32[512]{0:T(512)S(1)} %copy-done.33, f32[512]{0:T(512)S(1)} %copy-done.35, ...), kind=kLoop, calls=%fused_computation.74 | loop fusion | flops 15728640 | bytes 12605440 | tf_op jit(solution)/shard_map/add | solution.py:115
  585.5 132.9 %reduce-scatter.39.cloned.1.call-done = f32[16,2]{1,0:T(8,128)} async-done(((f32[512,2]{1,0:T(8,128)}), f32[16,2]{1,0:T(8,128)}) %reduce-scatter.39.cloned.1.call-update) | async-done | bytes 144
  719.2 133.0 %reduce-scatter.37.cloned.1.call-done = f32[16,2]{1,0:T(8,128)} async-done(((f32[512,2]{1,0:T(8,128)}), f32[16,2]{1,0:T(8,128)}) %reduce-scatter.37.cloned.1.call-update) | async-done | bytes 144
  852.9 133.0 %reduce-scatter.41.cloned.1.call-done = f32[16,2]{1,0:T(8,128)} async-done(((f32[512,2]{1,0:T(8,128)}), f32[16,2]{1,0:T(8,128)}) %reduce-scatter.41.cloned.1.call-update) | async-done | bytes 144
  987.3 132.4 %reduce-scatter.31.cloned.1.call-done = f32[16,7]{1,0:T(8,128)} async-done(((f32[512,7]{1,0:T(8,128)}), f32[16,7]{1,0:T(8,128)}) %reduce-scatter.31.cloned.1.call-update) | async-done | bytes 464
  1120.4 132.8 %reduce-scatter.33.cloned.1.call-done = f32[16,7]{1,0:T(8,128)} async-done(((f32[512,7]{1,0:T(8,128)}), f32[16,7]{1,0:T(8,128)}) %reduce-scatter.33.cloned.1.call-update) | async-done | bytes 464
  1254.6 102.0 %reduce-scatter.27.cloned.1.call-done = f32[48,512]{1,0:T(8,128)} async-done(((f32[1536,512]{1,0:T(8,128)}), f32[48,512]{1,0:T(8,128)}) %reduce-scatter.27.cloned.1.call-update) | async-done | bytes 98320 | tf_op jit(solution)/shard_map/reduce_scatter | solution.py:198
  1356.6 106.4 %reduce-scatter.29.cloned.1.call-done = f32[48,512]{1,0:T(8,128)} async-done(((f32[1536,512]{1,0:T(8,128)}), f32[48,512]{1,0:T(8,128)}) %reduce-scatter.29.cloned.1.call-update) | async-done | bytes 98320 | tf_op jit(solution)/shard_map/reduce_scatter | solution.py:198
  1464.7 104.9 %reduce-scatter.25.cloned.1.call-done = f32[16,1536]{1,0:T(8,128)} async-done(((f32[512,1536]{1,0:T(8,128)}), f32[16,1536]{1,0:T(8,128)}) %reduce-scatter.25.cloned.1.call-update) | async-done | bytes 98320 | tf_op jit(solution)/shard_map/reduce_scatter | solution.py:196
  1569.6 106.4 %reduce-scatter.23.cloned.1.call-done = f32[16,1536]{1,0:T(8,128)} async-done(((f32[512,1536]{1,0:T(8,128)}), f32[16,1536]{1,0:T(8,128)}) %reduce-scatter.23.cloned.1.call-update) | async-done | bytes 98320 | tf_op jit(solution)/shard_map/reduce_scatter | solution.py:196
  (273 shorter events, 155.1 us)
Async XLA Ops:
  7.2 268.6 %all-gather.21.cloned.1.call-start = ((), (), s32[]{:S(2)}) async-start(), calls=%async_computation.14 | async-start | bytes 1622016 | tf_op jit(solution)/shard_map/all_gather | solution.py:165
  8.9 300.0 %all-gather.23.cloned.1.call-start = ((), (), s32[]{:S(2)}) async-start(), calls=%async_computation.15 | async-start | bytes 1622016 | tf_op jit(solution)/shard_map/all_gather | solution.py:167
  10.4 314.5 %all-gather.25.cloned.1.call-start = ((), (), s32[]{:S(2)}) async-start(), calls=%async_computation.16 | async-start | bytes 1622016 | tf_op jit(solution)/shard_map/all_gather | solution.py:165
  11.1 348.0 %all-gather.27.cloned.1.call-start = ((), (), s32[]{:S(2)}) async-start(), calls=%async_computation.17 | async-start | bytes 1622016 | tf_op jit(solution)/shard_map/all_gather | solution.py:167
  11.9 242.7 %collective-permute-start = (bf16[1,2,16]{2,1,0:T(2,128)(2,1)S(1)}, bf16[1,2,16]{2,1,0:T(2,128)(2,1)S(1)}, u32[]{:S(2)}, u32[]{:S(2)}) collective-permute-start(bf16[1,2,16]{2,1,0:T(2,128)(2,1)S(1)} %get-tuple-element.139), channel_id=1, source_target_pairs={{0,1},{1,0},{2,3},{3,2},{4,5},{5,4},{6,7},{7,6},{8,9},{9,8},{10,11... | collective-permute-start | bytes 200 | tf_op jit(solution)/shard_map/ppermute | solution.py:21
  12.4 243.7 %collective-permute-start.5 = (bf16[1,2,16]{2,1,0:T(2,128)(2,1)S(1)}, bf16[1,2,16]{2,1,0:T(2,128)(2,1)S(1)}, u32[]{:S(2)}, u32[]{:S(2)}) collective-permute-start(bf16[1,2,16]{2,1,0:T(2,128)(2,1)S(1)} %get-tuple-element.138), channel_id=1, source_target_pairs={{0,1},{1,0},{2,3},{3,2},{4,5},{5,4},{6,7},{7,6},{8,9},{9,8},{10,11... | collective-permute-start | bytes 200 | tf_op jit(solution)/shard_map/ppermute | solution.py:21
  12.4 572.3 %reduce-scatter.35.cloned.1.call-start = ((), (), s32[]{:S(2)}) async-start(), calls=%async_computation.20 | async-start | bytes 270336
  254.6 3.6 collective-permute-start.1
  256.1 3.6 collective-permute-start.6
  258.3 3.7 collective-permute-start.2
  259.8 3.7 collective-permute-start.7
  262.0 3.7 collective-permute-start.3
  263.5 3.7 collective-permute-start.8
  265.7 4.6 collective-permute-start.4
  267.2 4.6 collective-permute-start.9
  450.8 267.6 %reduce-scatter.39.cloned.1.call-start = ((), (), s32[]{:S(2)}) async-start(), calls=%async_computation.22 | async-start | bytes 270336
  454.3 397.9 %reduce-scatter.37.cloned.1.call-start = ((), (), s32[]{:S(2)}) async-start(), calls=%async_computation.21 | async-start | bytes 270336
  455.1 530.8 %reduce-scatter.41.cloned.1.call-start = ((), (), s32[]{:S(2)}) async-start(), calls=%async_computation.23 | async-start | bytes 270336
  455.8 663.9 %reduce-scatter.31.cloned.1.call-start = ((), (), s32[]{:S(2)}) async-start(), calls=%async_computation.18 | async-start | bytes 270336
  480.5 772.7 %reduce-scatter.33.cloned.1.call-start = ((), (), s32[]{:S(2)}) async-start(), calls=%async_computation.19 | async-start | bytes 270336
  481.5 875.1 %reduce-scatter.27.cloned.1.call-start = ((), (), s32[]{:S(2)}) async-start(), calls=%async_computation.12 | async-start | bytes 3244032 | tf_op jit(solution)/shard_map/reduce_scatter | solution.py:198
  490.3 972.8 %reduce-scatter.29.cloned.1.call-start = ((), (), s32[]{:S(2)}) async-start(), calls=%async_computation.13 | async-start | bytes 3244032 | tf_op jit(solution)/shard_map/reduce_scatter | solution.py:198
  498.4 1071.1 %reduce-scatter.25.cloned.1.call-start = ((), (), s32[]{:S(2)}) async-start(), calls=%async_computation.11 | async-start | bytes 3244032 | tf_op jit(solution)/shard_map/reduce_scatter | solution.py:196
  507.3 1168.7 %reduce-scatter.23.cloned.1.call-start = ((), (), s32[]{:S(2)}) async-start(), calls=%async_computation.10 | async-start | bytes 3244032 | tf_op jit(solution)/shard_map/reduce_scatter | solution.py:196
  (46 other events, 1201.1 us)
Sparse Core Ops, SparseCore 0:
  11.4 57.6 all-gather.20
  72.0 53.9 all-gather.22
  129.4 54.2 all-gather.24
  187.0 53.7 all-gather.26
  450.9 133.7 reduce-scatter.34
  586.8 131.5 reduce-scatter.38
  720.6 131.4 reduce-scatter.36
  854.4 131.4 reduce-scatter.40
  988.1 131.4 reduce-scatter.30
  1121.7 131.4 reduce-scatter.32
  1258.7 97.9 reduce-scatter.26
  1361.9 101.0 reduce-scatter.28
  1468.5 101.0 reduce-scatter.24
  1574.9 101.0 reduce-scatter.22
